TPU v7x, 32 devices: a whole 2x2x4 slice. The times are simulated.
32 devices in a mesh: row: 8 (over z, x), col: 4 (over y, core).
Axes of the slice: x: 2, y: 2, z: 4, core: 2. Of those that a mesh axis runs over, the one named last changes fastest.
Arguments:
- momentum: bfloat16 [16384, 16384], P('row', 'col'), may hold values from -16 to 16
- gradient: bfloat16 [16384, 16384], P('row', 'col'), may hold values from -6 to 6
- right_basis: bfloat16 [1024, 16384], P('row', 'col'), may hold values from -1 to 1
Outputs:
- momentum_next: bfloat16 [16384, 16384], P('row', 'col')
- basis_next: float32 [1024, 16384], P('row', 'col')
- update: bfloat16 [16384, 16384], P('row', 'col')
All inputs are finite; a program needn't handle non-finite values.
Results may differ from a plain program's by a relative error of at most 0.02.
Values may be sent and summed in bfloat16 or wider, within the bound.
A program may use at most 128 MiB of HBM per device.

v0:
```python
import math
import jax
import jax.numpy as jnp
from jax import lax
from jax.sharding import PartitionSpec as P

D = 16384
RANK = 1024
momentum_decay = 0.95
epsilon = 1e-06


def orthonormalize(projected, gram_matrix):
    lower_factor = jnp.linalg.cholesky(gram_matrix)
    solved = jax.scipy.linalg.solve_triangular(lower_factor, projected.T, lower=True)
    return solved.T.astype(jnp.bfloat16)


def self_gram(projected):
    return lax.dot_general(
        projected, projected, (((0,), (0,)), ((), ())), precision=lax.Precision.HIGHEST
    )


def body(momentum, gradient, right_basis):
    buffer = (momentum.astype(jnp.float32) + gradient.astype(jnp.float32)).astype(jnp.bfloat16)
    rank_rows = right_basis.shape[0]
    partial_value = lax.dot_general(
        buffer,
        lax.all_gather(right_basis, "row", axis=0, tiled=True),
        (((1,), (1,)), ((), ())),
        preferred_element_type=jnp.float32,
    )
    row_share = lax.psum_scatter(
        partial_value.astype(jnp.bfloat16), "col", scatter_dimension=0, tiled=True
    ).astype(jnp.float32)
    gram_matrix = lax.psum(self_gram(row_share), ("row", "col"))
    ortho_share = orthonormalize(row_share, gram_matrix)
    orthonormal = lax.all_gather(ortho_share, "col", axis=0, tiled=True)
    right_share = lax.psum_scatter(
        lax.dot_general(
            orthonormal, buffer, (((0,), (0,)), ((), ())), preferred_element_type=jnp.float32
        ).astype(jnp.bfloat16),
        "row",
        scatter_dimension=0,
        tiled=True,
    )
    right_wide = right_share.astype(jnp.float32)
    gathered = lax.all_gather(right_share, "row", axis=0, tiled=True)
    gathered_wide = gathered.astype(jnp.float32)
    sums_total = lax.psum(jnp.sum(gathered_wide * gathered_wide, axis=1), "col")
    inverse_norm = lax.rsqrt(sums_total + epsilon)[:, None]
    scaled = (gathered_wide * inverse_norm).astype(jnp.bfloat16)
    feedback = jnp.dot(orthonormal, gathered, preferred_element_type=jnp.float32)
    direction = jnp.dot(orthonormal, scaled, preferred_element_type=jnp.float32)
    offset = lax.axis_index("row") * rank_rows
    basis_next = right_wide * lax.dynamic_slice_in_dim(inverse_norm, offset, rank_rows, 0)
    momentum_next = (buffer.astype(jnp.float32) - (1.0 - momentum_decay) * feedback).astype(
        jnp.bfloat16
    )
    update_scale = D / math.sqrt(RANK)
    update = (update_scale * direction).astype(jnp.bfloat16)
    return (momentum_next, basis_next, update)


def solution(mesh):
    return jax.shard_map(
        body,
        mesh=mesh,
        in_specs=(P("row", "col"), P("row", "col"), P("row", "col")),
        out_specs=(P("row", "col"), P("row", "col"), P("row", "col")),
        check_vma=False,
    )
```

profile of v0, /device:TPU:0, one launch (start us, length us, event | category | flops | bytes accessed | tf_op | source)
XLA Modules:
  0.0 1132.3 jit_solution(6209591932826324028)
XLA Ops:
  7.9 129.4 %all-gather.4.cloned.1.call-done = bf16[1024,4096]{1,0:T(8,128)(2,1)} async-done(((bf16[128,4096]{1,0:T(8,128)(2,1)}), bf16[1024,4096]{1,0:T(8,128)(2,1)}) %all-gather.4.cloned.1.call-update) | async-done | bytes 8388624 | tf_op jit(solution)/shard_map/all_gather | solution.py:30
  137.3 25.8 %convolution_convert_fusion.1 = bf16[2048,1024]{1,0:T(8,128)(2,1)} fusion(bf16[1024,4096]{1,0:T(8,128)(2,1)} %all-gather.4.cloned.1.call-done, bf16[2048,4096]{1,0:T(8,128)(2,1)} %param.4, bf16[2048,4096]{1,0:T(8,128)(2,1)} %param.3), kind=kOutput, calls=%fused_computation.15 | convolution fusion | flops 17215520768 | bytes 46137344 | tf_op jit(solution)/shard_map/dot_general | solution.py:28
  163.2 42.9 %reduce-scatter.3.cloned.1.call-done = bf16[512,1024]{1,0:T(8,128)(2,1)} async-done(((bf16[2048,1024]{1,0:T(8,128)(2,1)}), bf16[512,1024]{1,0:T(8,128)(2,1)}) %reduce-scatter.3.cloned.1.call-update) | async-done | bytes 1048592 | tf_op jit(solution)/shard_map/reduce_scatter | solution.py:34
  206.1 4.9 fusion.67
  211.3 143.2 %all-reduce.3.cloned.1.call-done = f32[1024,1024]{0,1:T(8,128)} async-done(((f32[1024,1024]{0,1:T(8,128)}), f32[1024,1024]{0,1:T(8,128)}) %all-reduce.3.cloned.1.call-update) | async-done | bytes 4194320 | tf_op jit(solution)/shard_map/psum | solution.py:37
  354.5 5.5 copy.7
  360.0 4.4 fusion.4
  364.5 2.0 copy-done.1
  366.5 11.7 %cholesky.223 = f32[128,128]{1,0:T(8,128)S(1)} custom-call(f32[128,128]{1,0:T(8,128)S(1)} %cholesky.580), custom_call_target="Cholesky" | custom-call | tf_op jit(solution)/shard_map/jit(cholesky)/cholesky | solution.py:14
  378.2 9.8 custom-call.63
  388.1 2.5 cholesky.255
  390.6 2.3 constant_dynamic-update-slice_fusion.25
  392.9 1.5 convolution_subtract_fusion
  395.2 12.1 %cholesky.244 = f32[128,128]{1,0:T(8,128)S(1)} custom-call(f32[128,128]{1,0:T(8,128)S(1)} %cholesky.584), custom_call_target="Cholesky" | custom-call | tf_op jit(solution)/shard_map/jit(cholesky)/cholesky | solution.py:14
  408.0 9.8 custom-call.64
  417.8 2.2 convolution_dynamic-update-slice_fusion
  420.0 2.1 convolution_subtract_fusion.1
  422.7 13.2 %cholesky.468 = f32[128,128]{1,0:T(8,128)} custom-call(f32[128,128]{1,0:T(8,128)} %cholesky.589), custom_call_target="Cholesky" | custom-call | tf_op jit(solution)/shard_map/jit(cholesky)/cholesky | solution.py:14
  435.9 1.5 select_reduce_fusion.5
  438.0 11.3 custom-call.65
  449.3 2.0 convolution_dynamic-update-slice_fusion.1
  451.2 2.3 convolution_subtract_fusion.2
  453.6 12.5 %cholesky.487 = f32[128,128]{1,0:T(8,128)} custom-call(f32[128,128]{1,0:T(8,128)S(1)} %cholesky.594), custom_call_target="Cholesky" | custom-call | tf_op jit(solution)/shard_map/jit(cholesky)/cholesky | solution.py:14
  468.2 10.4 custom-call.66
  478.6 1.9 convolution_dynamic-update-slice_fusion.2
  480.6 2.3 convolution_subtract_fusion.10
  482.9 11.7 %cholesky.506 = f32[128,128]{1,0:T(8,128)S(1)} custom-call(f32[128,128]{1,0:T(8,128)S(1)} %cholesky.599), custom_call_target="Cholesky" | custom-call | tf_op jit(solution)/shard_map/jit(cholesky)/cholesky | solution.py:14
  495.9 10.0 custom-call.67
  506.9 2.3 convolution_subtract_fusion.11
  509.2 11.7 %cholesky.526 = f32[128,128]{1,0:T(8,128)S(1)} custom-call(f32[128,128]{1,0:T(8,128)S(1)} %cholesky.604), custom_call_target="Cholesky" | custom-call | tf_op jit(solution)/shard_map/jit(cholesky)/cholesky | solution.py:14
  522.2 9.8 custom-call.68
  532.9 2.1 convolution_subtract_fusion.12
  535.0 12.0 %cholesky.546 = f32[128,128]{1,0:T(8,128)S(1)} custom-call(f32[128,128]{1,0:T(8,128)S(1)} %cholesky.609), custom_call_target="Cholesky" | custom-call | tf_op jit(solution)/shard_map/jit(cholesky)/cholesky | solution.py:14
  548.4 9.8 custom-call.69
  559.1 1.8 convolution_subtract_fusion.13
  560.9 11.7 %cholesky.564 = f32[128,128]{1,0:T(8,128)S(1)} custom-call(f32[128,128]{1,0:T(8,128)S(1)} %convolution_subtract_fusion.13), custom_call_target="Cholesky" | custom-call | tf_op jit(solution)/shard_map/jit(cholesky)/cholesky | solution.py:14
  579.5 4.9 select_select_fusion
  584.4 29.0 %while.1 = (s32[]{:T(128)}, f32[1024,1024]{1,0:T(8,128)}, s32[8,2]{0,1:T(2,128)S(1)}, f32[8,128,128]{2,1,0:T(8,128)}, s32[]{:T(128)}) while((s32[]{:T(128)}, f32[1024,1024]{1,0:T(8,128)}, s32[8,2]{0,1:T(2,128)S(1)}, f32[8,128,128]{2,1,0:T(8,128)}, s32[]{:T(128)}) %tuple.57), condition=%wide.while_cond, body=%wide.while_body.sunk | while | flops 2 | bytes 132205 | solution.py:15
  585.1 3.0 bitcast_dynamic-update-slice_fusion.2
  588.7 3.0 bitcast_dynamic-update-slice_fusion.2
  592.3 3.0 bitcast_dynamic-update-slice_fusion.2
  596.0 3.0 bitcast_dynamic-update-slice_fusion.2
  599.6 3.0 bitcast_dynamic-update-slice_fusion.2
  603.2 3.0 bitcast_dynamic-update-slice_fusion.2
  606.9 3.0 bitcast_dynamic-update-slice_fusion.2
  610.5 2.9 bitcast_dynamic-update-slice_fusion.2
  613.4 80.2 %custom-call.70 = f32[8,128,128]{1,2,0:T(8,128)} custom-call(f32[8,128,128]{2,1,0:T(8,128)} %get-tuple-element.10), custom_call_target="InvertDiagBlocksLowerTriangular" | custom-call | tf_op jit(solution)/shard_map/jit(_solve_triangular)/triangular_solve | solution.py:15
  693.6 1.9 convert_dynamic-update-slice_fusion.6
  697.0 1.9 convert_dynamic-update-slice_fusion.5
  699.0 1.9 convolution_subtract_fusion.5
  702.0 2.4 convolution_subtract_fusion.8
  705.4 2.8 convolution_subtract_fusion.9
  709.7 3.2 convolution_subtract_fusion.4
  714.0 3.6 convolution_subtract_fusion.7
  718.8 4.3 convolution_subtract_fusion.3
  724.2 33.9 %all-gather.6.cloned.1.call-done = bf16[2048,1024]{0,1:T(8,128)(2,1)} async-done(((bf16[512,1024]{0,1:T(8,128)(2,1)}), bf16[2048,1024]{0,1:T(8,128)(2,1)}) %all-gather.6.cloned.1.call-update) | async-done | bytes 4194320 | tf_op jit(solution)/shard_map/all_gather | solution.py:39
  758.1 24.2 %convolution_convert_fusion = bf16[1024,4096]{1,0:T(8,128)(2,1)} fusion(bf16[2048,1024]{0,1:T(8,128)(2,1)} %all-gather.6.cloned.1.call-done, bf16[2048,4096]{1,0:T(8,128)(2,1)} %param.4, bf16[2048,4096]{1,0:T(8,128)(2,1)} %param.3), kind=kOutput, calls=%fused_computation.10 | convolution fusion | flops 17217617920 | bytes 46137344 | tf_op jit(solution)/shard_map/dot_general | solution.py:41
  782.3 147.5 %reduce-scatter.5.cloned.1.call-done = bf16[128,4096]{1,0:T(8,128)(2,1)} async-done(((bf16[1024,4096]{1,0:T(8,128)(2,1)}), bf16[128,4096]{1,0:T(8,128)(2,1)}) %reduce-scatter.5.cloned.1.call-update) | async-done | bytes 1048592 | tf_op jit(solution)/shard_map/reduce_scatter | solution.py:40
  929.9 125.6 %all-gather.8.cloned.1.call-done = bf16[1024,4096]{1,0:T(8,128)(2,1)} async-done(((bf16[128,4096]{1,0:T(8,128)(2,1)}), bf16[1024,4096]{1,0:T(8,128)(2,1)}) %all-gather.8.cloned.1.call-update) | async-done | bytes 8388624 | tf_op jit(solution)/shard_map/all_gather | solution.py:49
  1055.5 5.1 fusion
  1060.5 5.9 psum.15
  1066.5 26.4 %multiply_convert_fusion = bf16[2048,4096]{1,0:T(8,128)(2,1)} fusion(bf16[2048,1024]{0,1:T(8,128)(2,1)} %all-gather.6.cloned.1.call-done, bf16[1024,4096]{1,0:T(8,128)(2,1)} %all-gather.8.cloned.1.call-done, f32[1024]{0:T(1024)S(1)} %add_rsqrt_fusion), kind=kOutput, calls=%fused_computation.2 | convolution fusion | flops 17209229312 | bytes 29364224 | tf_op jit(solution)/shard_map/dot_general | solution.py:55
  1092.9 30.5 %subtract_convert_fusion = bf16[2048,4096]{1,0:T(8,128)(2,1)} fusion(bf16[2048,1024]{0,1:T(8,128)(2,1)S(1)} %copy-done.5, bf16[1024,4096]{1,0:T(8,128)(2,1)} %all-gather.8.cloned.1.call-done, bf16[2048,4096]{1,0:T(8,128)(2,1)} %param.4, bf16[2048,4096]{1,0:T(8,128)(2,1)} %param.3), kind=kOutput, calls=%fused_computation.3 | convolution fusion | flops 17246978048 | bytes 62914560 | tf_op jit(solution)/shard_map/dot_general | solution.py:54
  1123.4 1.6 convert_multiply_fusion.2
  (83 shorter events, 28.7 us)
Async XLA Ops:
  7.2 130.2 %all-gather.4.cloned.1.call-start = ((), (), s32[]{:S(2)}) async-start(), calls=%async_computation.2 | async-start | bytes 9437184 | tf_op jit(solution)/shard_map/all_gather | solution.py:30
  7.9 198.2 %reduce-scatter.3.cloned.1.call-start = ((), (), s32[]{:S(2)}) async-start(), calls=%async_computation.3 | async-start | bytes 5242880 | tf_op jit(solution)/shard_map/reduce_scatter | solution.py:34
  163.1 191.4 %all-reduce.3.cloned.1.call-start = ((), (), s32[]{:S(2)}) async-start(), calls=%async_computation.4 | async-start | bytes 8388608 | tf_op jit(solution)/shard_map/psum | solution.py:37
  206.1 5.0 copy-start
  211.0 547.1 %all-gather.6.cloned.1.call-start = ((), (), s32[]{:S(2)}) async-start(), calls=%async_computation.5 | async-start | bytes 5242880 | tf_op jit(solution)/shard_map/all_gather | solution.py:39
  364.5 2.0 copy-start.1
  394.5 0.8 copy-start.3
  693.6 7.2 copy-start.4
  724.2 205.7 %reduce-scatter.5.cloned.1.call-start = ((), (), s32[]{:S(2)}) async-start(), calls=%async_computation.6 | async-start | bytes 9437184 | tf_op jit(solution)/shard_map/reduce_scatter | solution.py:40
  782.3 273.2 %all-gather.8.cloned.1.call-start = ((), (), s32[]{:S(2)}) async-start(), calls=%async_computation.7 | async-start | bytes 9437184 | tf_op jit(solution)/shard_map/all_gather | solution.py:49
  1066.5 26.4 %copy-start.5 = (bf16[2048,1024]{0,1:T(8,128)(2,1)S(1)}, bf16[2048,1024]{0,1:T(8,128)(2,1)}, u32[]{:S(2)}) copy-start(bf16[2048,1024]{0,1:T(8,128)(2,1)} %all-gather.6.cloned.1.call-done) | copy-start | bytes 12582916
  1092.9 30.5 %copy-start.2 = (bf16[128,4096]{1,0:T(8,128)(2,1)S(1)}, bf16[128,4096]{1,0:T(8,128)(2,1)}, u32[]{:S(2)}) copy-start(bf16[128,4096]{1,0:T(8,128)(2,1)} %reduce-scatter.5.cloned.1.call-done) | copy-start | bytes 3145732
Sparse Core Ops, SparseCore 0:
  10.1 127.1 all-gather.3
  163.3 42.7 reduce-scatter.2
  212.2 142.2 all-reduce.2
  724.3 33.7 all-gather.5
  782.4 147.4 reduce-scatter.4
  931.9 123.5 all-gather.7
where the time goes:
time: 1140 us; the launch traced here: 1130 us
  waiting for transfers between devices  623 us (55%)
  other arithmetic  275 us (24%)
  matrix products  167 us (15%)
  local copies, waits for them, and re-layouts  41.1 us (4%)
  between operations  19.9 us (2%)
    another operation x30, other arithmetic, orthonormalize(): lower_factor = jnp.linalg.cholesky(gram_matrix)  178 us
    reduce_scatter x1, waiting for transfers between devices, body(): lax.psum_scatter(lax.dot_general(orthonormal, buffer, (((0,), (0,)), ((),...  148 us
    psum x1, waiting for transfers between devices, body(): gram_matrix = lax.psum(self_gram(row_share), ('row', 'col'))  143 us
    all_gather x1, waiting for transfers between devices, body(): lax.all_gather(right_basis, 'row', axis=0, tiled=True)  129 us
    all_gather x1, waiting for transfers between devices, body(): gathered = lax.all_gather(right_share, 'row', axis=0, tiled=True)  126 us
    another operation x3, other arithmetic, orthonormalize(): jax.scipy.linalg.solve_triangular(lower_factor, projected.T, lower=True)  85.1 us
    reduce_scatter x1, waiting for transfers between devices, body(): lax.psum_scatter(partial_value.astype(jnp.bfloat16), 'col', scatter_dimen...  42.9 us
    all_gather x1, waiting for transfers between devices, body(): orthonormal = lax.all_gather(ortho_share, 'col', axis=0, tiled=True)  33.9 us
  transfers between devices with their start and end apart: 6, of which 6 were waited for; matrix products, arithmetic and copies ran while one was open for 0% of the time, Pallas kernels for 0%

commit v1 on v0

--- a/solution.py
+++ b/solution.py
@@ -34,7 +34,7 @@
     row_share = lax.psum_scatter(
         partial_value.astype(jnp.bfloat16), "col", scatter_dimension=0, tiled=True
     ).astype(jnp.float32)
-    gram_matrix = lax.psum(self_gram(row_share), ("row", "col"))
+    gram_matrix = lax.psum(lax.psum(self_gram(row_share), "col"), "row")
     ortho_share = orthonormalize(row_share, gram_matrix)
     orthonormal = lax.all_gather(ortho_share, "col", axis=0, tiled=True)
     right_share = lax.psum_scatter(

time: 1140 us -> 1240 us (1.088)
  waiting for transfers between devices: 623 us -> 725 us
    psum x1 -> x2, waiting for transfers between devices: 143 us -> 245 us  [body(): gram_matrix = lax.psum(lax.psum(self_gram(row_share), 'col'), 'row')]
  transfers between devices with their start and end apart: 6 -> 7, of which waited for: 6 -> 7; matrix products, arithmetic and copies ran while one was open for 0% -> 0% of each run, Pallas kernels for 0% -> 0%
where the time goes in v1:
time: 1240 us; the launch traced here: 1230 us
  waiting for transfers between devices  725 us (58%)
  other arithmetic  275 us (22%)
  matrix products  167 us (13%)
  local copies, waits for them, and re-layouts  41.1 us (3%)
  between operations  19.9 us (2%)
    psum x2, waiting for transfers between devices, body(): gram_matrix = lax.psum(lax.psum(self_gram(row_share), 'col'), 'row')  245 us
    another operation x30, other arithmetic, orthonormalize(): lower_factor = jnp.linalg.cholesky(gram_matrix)  178 us
    reduce_scatter x1, waiting for transfers between devices, body(): lax.psum_scatter(lax.dot_general(orthonormal, buffer, (((0,), (0,)), ((),...  148 us
    all_gather x1, waiting for transfers between devices, body(): lax.all_gather(right_basis, 'row', axis=0, tiled=True)  129 us
    all_gather x1, waiting for transfers between devices, body(): gathered = lax.all_gather(right_share, 'row', axis=0, tiled=True)  126 us
    another operation x3, other arithmetic, orthonormalize(): jax.scipy.linalg.solve_triangular(lower_factor, projected.T, lower=True)  85.1 us
    reduce_scatter x1, waiting for transfers between devices, body(): lax.psum_scatter(partial_value.astype(jnp.bfloat16), 'col', scatter_dimen...  42.9 us
    all_gather x1, waiting for transfers between devices, body(): orthonormal = lax.all_gather(ortho_share, 'col', axis=0, tiled=True)  33.6 us
  transfers between devices with their start and end apart: 7, of which 7 were waited for; matrix products, arithmetic and copies ran while one was open for 0% of the time, Pallas kernels for 0%

profile of v1, /device:TPU:0, one launch (start us, length us, event | category | flops | bytes accessed | tf_op | source)
XLA Modules:
  0.0 1234.6 jit_solution(17225268542202197646)
XLA Ops:
  7.9 129.4 %all-gather.4.cloned.1.call-done = bf16[1024,4096]{1,0:T(8,128)(2,1)} async-done(((bf16[128,4096]{1,0:T(8,128)(2,1)}), bf16[1024,4096]{1,0:T(8,128)(2,1)}) %all-gather.4.cloned.1.call-update) | async-done | bytes 8388624 | tf_op jit(solution)/shard_map/all_gather | solution.py:30
  137.3 25.8 %convolution_convert_fusion.1 = bf16[2048,1024]{1,0:T(8,128)(2,1)} fusion(bf16[1024,4096]{1,0:T(8,128)(2,1)} %all-gather.4.cloned.1.call-done, bf16[2048,4096]{1,0:T(8,128)(2,1)} %param.4, bf16[2048,4096]{1,0:T(8,128)(2,1)} %param.3), kind=kOutput, calls=%fused_computation.15 | convolution fusion | flops 17215520768 | bytes 46137344 | tf_op jit(solution)/shard_map/dot_general | solution.py:28
  163.2 42.9 %reduce-scatter.3.cloned.1.call-done = bf16[512,1024]{1,0:T(8,128)(2,1)} async-done(((bf16[2048,1024]{1,0:T(8,128)(2,1)}), bf16[512,1024]{1,0:T(8,128)(2,1)}) %reduce-scatter.3.cloned.1.call-update) | async-done | bytes 1048592 | tf_op jit(solution)/shard_map/reduce_scatter | solution.py:34
  206.1 5.0 fusion.67
  211.2 85.6 %all-reduce.4.cloned.1.call-done = f32[1024,1024]{0,1:T(8,128)} async-done(((f32[1024,1024]{0,1:T(8,128)}), f32[1024,1024]{0,1:T(8,128)}) %all-reduce.4.cloned.1.call-update) | async-done | bytes 4194320 | tf_op jit(solution)/shard_map/psum | solution.py:37
  297.1 159.8 %all-reduce.6.cloned.1.call-done = f32[1024,1024]{0,1:T(8,128)} async-done(((f32[1024,1024]{0,1:T(8,128)}), f32[1024,1024]{0,1:T(8,128)}) %all-reduce.6.cloned.1.call-update) | async-done | bytes 4194320 | tf_op jit(solution)/shard_map/psum | solution.py:37
  456.9 5.5 copy.7
  462.4 4.4 fusion.4
  466.9 2.0 copy-done.1
  468.9 11.7 cholesky.223
  480.6 9.8 custom-call.63
  490.4 2.5 cholesky.255
  493.0 2.3 constant_dynamic-update-slice_fusion.25
  495.3 1.5 convolution_subtract_fusion
  497.6 12.1 cholesky.244
  510.3 9.8 custom-call.64
  520.1 2.2 convolution_dynamic-update-slice_fusion
  522.4 2.1 convolution_subtract_fusion.1
  525.1 13.2 %cholesky.468 = f32[128,128]{1,0:T(8,128)} custom-call(f32[128,128]{1,0:T(8,128)} %cholesky.589), custom_call_target="Cholesky" | custom-call | tf_op jit(solution)/shard_map/jit(cholesky)/cholesky | solution.py:14
  540.4 11.3 custom-call.65
  551.6 2.0 convolution_dynamic-update-slice_fusion.1
  553.6 2.3 convolution_subtract_fusion.2
  556.0 12.5 %cholesky.487 = f32[128,128]{1,0:T(8,128)} custom-call(f32[128,128]{1,0:T(8,128)S(1)} %cholesky.594), custom_call_target="Cholesky" | custom-call | tf_op jit(solution)/shard_map/jit(cholesky)/cholesky | solution.py:14
  570.6 10.4 custom-call.66
  581.0 1.9 convolution_dynamic-update-slice_fusion.2
  582.9 2.3 convolution_subtract_fusion.10
  585.3 11.7 cholesky.506
  598.3 10.0 custom-call.67
  609.3 2.3 convolution_subtract_fusion.11
  611.6 11.7 cholesky.526
  624.5 9.8 custom-call.68
  635.3 2.1 convolution_subtract_fusion.12
  637.4 12.0 cholesky.546
  650.8 9.8 custom-call.69
  661.4 1.8 convolution_subtract_fusion.13
  663.2 11.7 cholesky.564
  681.9 4.9 select_select_fusion
  686.8 29.0 %while.1 = (s32[]{:T(128)}, f32[1024,1024]{1,0:T(8,128)}, s32[8,2]{0,1:T(2,128)S(1)}, f32[8,128,128]{2,1,0:T(8,128)}, s32[]{:T(128)}) while((s32[]{:T(128)}, f32[1024,1024]{1,0:T(8,128)}, s32[8,2]{0,1:T(2,128)S(1)}, f32[8,128,128]{2,1,0:T(8,128)}, s32[]{:T(128)}) %tuple.57), condition=%wide.while_cond, body=%wide.while_body.sunk | while | flops 2 | bytes 132205 | solution.py:15
  687.4 3.0 bitcast_dynamic-update-slice_fusion.2
  691.1 3.0 bitcast_dynamic-update-slice_fusion.2
  694.7 3.0 bitcast_dynamic-update-slice_fusion.2
  698.3 3.0 bitcast_dynamic-update-slice_fusion.2
  702.0 3.0 bitcast_dynamic-update-slice_fusion.2
  705.6 3.0 bitcast_dynamic-update-slice_fusion.2
  709.3 3.0 bitcast_dynamic-update-slice_fusion.2
  712.9 2.9 bitcast_dynamic-update-slice_fusion.2
  715.8 80.2 %custom-call.70 = f32[8,128,128]{1,2,0:T(8,128)} custom-call(f32[8,128,128]{2,1,0:T(8,128)} %get-tuple-element.10), custom_call_target="InvertDiagBlocksLowerTriangular" | custom-call | tf_op jit(solution)/shard_map/jit(_solve_triangular)/triangular_solve | solution.py:15
  796.0 1.9 convert_dynamic-update-slice_fusion.6
  799.4 1.9 convert_dynamic-update-slice_fusion.5
  801.3 1.9 convolution_subtract_fusion.5
  804.3 2.4 convolution_subtract_fusion.8
  807.8 2.8 convolution_subtract_fusion.9
  812.0 3.2 convolution_subtract_fusion.4
  816.4 3.6 convolution_subtract_fusion.7
  821.1 4.3 convolution_subtract_fusion.3
  826.6 33.6 %all-gather.6.cloned.1.call-done = bf16[2048,1024]{0,1:T(8,128)(2,1)} async-done(((bf16[512,1024]{0,1:T(8,128)(2,1)}), bf16[2048,1024]{0,1:T(8,128)(2,1)}) %all-gather.6.cloned.1.call-update) | async-done | bytes 4194320 | tf_op jit(solution)/shard_map/all_gather | solution.py:39
  860.2 24.2 %convolution_convert_fusion = bf16[1024,4096]{1,0:T(8,128)(2,1)} fusion(bf16[2048,1024]{0,1:T(8,128)(2,1)} %all-gather.6.cloned.1.call-done, bf16[2048,4096]{1,0:T(8,128)(2,1)} %param.4, bf16[2048,4096]{1,0:T(8,128)(2,1)} %param.3), kind=kOutput, calls=%fused_computation.10 | convolution fusion | flops 17217617920 | bytes 46137344 | tf_op jit(solution)/shard_map/dot_general | solution.py:41
  884.4 147.6 %reduce-scatter.5.cloned.1.call-done = bf16[128,4096]{1,0:T(8,128)(2,1)} async-done(((bf16[1024,4096]{1,0:T(8,128)(2,1)}), bf16[128,4096]{1,0:T(8,128)(2,1)}) %reduce-scatter.5.cloned.1.call-update) | async-done | bytes 1048592 | tf_op jit(solution)/shard_map/reduce_scatter | solution.py:40
  1032.0 125.7 %all-gather.8.cloned.1.call-done = bf16[1024,4096]{1,0:T(8,128)(2,1)} async-done(((bf16[128,4096]{1,0:T(8,128)(2,1)}), bf16[1024,4096]{1,0:T(8,128)(2,1)}) %all-gather.8.cloned.1.call-update) | async-done | bytes 8388624 | tf_op jit(solution)/shard_map/all_gather | solution.py:49
  1157.7 5.1 fusion
  1162.8 5.9 psum.23
  1168.8 26.4 %multiply_convert_fusion = bf16[2048,4096]{1,0:T(8,128)(2,1)} fusion(bf16[2048,1024]{0,1:T(8,128)(2,1)} %all-gather.6.cloned.1.call-done, bf16[1024,4096]{1,0:T(8,128)(2,1)} %all-gather.8.cloned.1.call-done, f32[1024]{0:T(1024)S(1)} %add_rsqrt_fusion), kind=kOutput, calls=%fused_computation.2 | convolution fusion | flops 17209229312 | bytes 29364224 | tf_op jit(solution)/shard_map/dot_general | solution.py:55
  1195.2 30.5 %subtract_convert_fusion = bf16[2048,4096]{1,0:T(8,128)(2,1)} fusion(bf16[2048,1024]{0,1:T(8,128)(2,1)S(1)} %copy-done.5, bf16[1024,4096]{1,0:T(8,128)(2,1)} %all-gather.8.cloned.1.call-done, bf16[2048,4096]{1,0:T(8,128)(2,1)} %param.4, bf16[2048,4096]{1,0:T(8,128)(2,1)} %param.3), kind=kOutput, calls=%fused_computation.3 | convolution fusion | flops 17246978048 | bytes 62914560 | tf_op jit(solution)/shard_map/dot_general | solution.py:54
  1225.7 1.6 convert_multiply_fusion.2
  (86 shorter events, 30.2 us)
Async XLA Ops:
  7.2 130.2 %all-gather.4.cloned.1.call-start = ((), (), s32[]{:S(2)}) async-start(), calls=%async_computation.2 | async-start | bytes 9437184 | tf_op jit(solution)/shard_map/all_gather | solution.py:30
  7.9 198.2 %reduce-scatter.3.cloned.1.call-start = ((), (), s32[]{:S(2)}) async-start(), calls=%async_computation.3 | async-start | bytes 5242880 | tf_op jit(solution)/shard_map/reduce_scatter | solution.py:34
  163.1 133.6 %all-reduce.4.cloned.1.call-start = ((), (), s32[]{:S(2)}) async-start(), calls=%async_computation.4 | async-start | bytes 8388608 | tf_op jit(solution)/shard_map/psum | solution.py:37
  211.1 85.8 %copy-start = (bf16[512,1024]{1,0:T(8,128)(2,1)S(1)}, bf16[512,1024]{1,0:T(8,128)(2,1)}, u32[]{:S(2)}) copy-start(bf16[512,1024]{1,0:T(8,128)(2,1)} %reduce-scatter.3.cloned.1.call-done) | copy-start | bytes 3145732
  211.1 245.8 %all-reduce.6.cloned.1.call-start = ((), (), s32[]{:S(2)}) async-start(), calls=%async_computation.5 | async-start | bytes 8388608 | tf_op jit(solution)/shard_map/psum | solution.py:37
  296.8 563.4 %all-gather.6.cloned.1.call-start = ((), (), s32[]{:S(2)}) async-start(), calls=%async_computation.6 | async-start | bytes 5242880 | tf_op jit(solution)/shard_map/all_gather | solution.py:39
  466.8 2.0 copy-start.1
  496.8 0.8 copy-start.3
  796.0 7.2 copy-start.4
  826.6 205.4 %reduce-scatter.5.cloned.1.call-start = ((), (), s32[]{:S(2)}) async-start(), calls=%async_computation.7 | async-start | bytes 9437184 | tf_op jit(solution)/shard_map/reduce_scatter | solution.py:40
  884.4 273.4 %all-gather.8.cloned.1.call-start = ((), (), s32[]{:S(2)}) async-start(), calls=%async_computation.8 | async-start | bytes 9437184 | tf_op jit(solution)/shard_map/all_gather | solution.py:49
  1168.8 26.4 %copy-start.5 = (bf16[2048,1024]{0,1:T(8,128)(2,1)S(1)}, bf16[2048,1024]{0,1:T(8,128)(2,1)}, u32[]{:S(2)}) copy-start(bf16[2048,1024]{0,1:T(8,128)(2,1)} %all-gather.6.cloned.1.call-done) | copy-start | bytes 12582916
  1195.2 30.5 %copy-start.2 = (bf16[128,4096]{1,0:T(8,128)(2,1)S(1)}, bf16[128,4096]{1,0:T(8,128)(2,1)}, u32[]{:S(2)}) copy-start(bf16[128,4096]{1,0:T(8,128)(2,1)} %reduce-scatter.5.cloned.1.call-done) | copy-start | bytes 3145732
Sparse Core Ops, SparseCore 0:
  10.1 127.1 all-gather.3
  163.3 42.7 reduce-scatter.2
  211.2 85.4 all-reduce.3
  300.3 156.5 all-reduce.5
  826.7 33.4 all-gather.5
  884.5 147.4 reduce-scatter.4
  1034.1 123.5 all-gather.7
